TPU v7x, 32 devices: a whole 2x2x4 slice. The times are simulated.
32 devices in a mesh: dp: 16 (over z, y, x), tensor: 2 (over core).
Axes of the slice: x: 2, y: 2, z: 4, core: 2. Of those that a mesh axis runs over, the one named last changes fastest.
Arguments:
- tokens: bfloat16 [32768, 768], P('dp'), may hold values from -6 to 6
- cotangent: bfloat16 [32768, 768], P('dp'), may hold values from -6 to 6
- seq_ids: int32 [32768], P('dp'), may hold values from 0 to 39, as said below
- block_slot: int32 [216], replicated, may hold values from 0 to 223, as said below
- masters: float32 [2, 224, 128, 128], P('tensor', 'dp')
- left_stats: float32 [2, 224, 128, 128], P('tensor', 'dp'), as said below
- right_stats: float32 [2, 224, 128, 128], P('tensor', 'dp'), as said below
- left_roots: float32 [2, 224, 128, 128], P('tensor', 'dp'), as said below
- right_roots: float32 [2, 224, 128, 128], P('tensor', 'dp'), as said below
- vectors: float32 [9984], replicated
- vector_momentum: float32 [9984], replicated, may hold values from -0.9 to 0.9
Outputs:
- mixed: bfloat16 [32768, 768], P(('dp', 'tensor'))
- input_grad: float32 [32768, 768], P(('dp', 'tensor'))
- matrix_grads: float32 [2, 224, 128, 128], P('tensor', 'dp')
- new_masters: float32 [2, 224, 128, 128], P('tensor', 'dp')
- new_left: float32 [2, 224, 128, 128], P('tensor', 'dp')
- new_right: float32 [2, 224, 128, 128], P('tensor', 'dp')
- new_vectors: float32 [9984], replicated
- new_vector_momentum: float32 [9984], replicated
Inputs may be any that keep to these rules, and one draw needn't show every extreme that they name: `seq_ids`: each aligned block of 2048 tokens holds either one sequence or 4 sequences of 512 tokens, half of the blocks of each kind; ids count the sequences in order from 0 and are equal within a sequence. `block_slot`: Distinct; slot s belongs to index s // 14 of dp; slots that no block names hold no block. `left_stats`: symmetric in each slot. `right_stats`: symmetric in each slot. `left_roots`: symmetric in each slot. `right_roots`: symmetric in each slot.
All inputs are finite; a program needn't handle non-finite values.
Results may differ from a plain program's by a relative error of at most 0.0095.
Values may be sent and summed in bfloat16 or wider, within the bound.
No kernel may reach another device: no remote copies, remote signals or barrier semaphores. Data moves between devices by JAX's collectives and lax.ppermute only.
A program may use at most 256 MiB of HBM per device.

v0:
```python
import jax
import jax.numpy as jnp
from jax import lax
from jax.sharding import PartitionSpec as P

H = 12
HD = 64
ROT = 16
FF = 3072
norm_eps = 1e-05
floor_score = -1e30
rate_matrix = 0.03
rate_vector = 1.5
decay_vector = 0.9


def contract(first_op, second_op, first_dim, second_dim):
    return lax.dot_general(
        first_op,
        second_op,
        (((first_dim,), (second_dim,)), ((), ())),
        preferred_element_type=jnp.float32,
    )


def unblock(blocks, row_total, col_total):
    blk_size = blocks.shape[-1]
    return (
        blocks.reshape(row_total // blk_size, col_total // blk_size, blk_size, blk_size)
        .transpose(0, 2, 1, 3)
        .reshape(row_total, col_total)
    )


def to_blocks(matrix, blk_size):
    row_count, col_count = matrix.shape
    return (
        matrix.reshape(row_count // blk_size, blk_size, col_count // blk_size, blk_size)
        .transpose(0, 2, 1, 3)
        .reshape(-1, blk_size, blk_size)
    )


def rotate(values, cosine_tab, sine_tab, local_heads):
    tok_rows = values.shape[0]
    shaped = values.reshape(tok_rows, local_heads, HD)
    rot_half = ROT // 2
    lower_half = shaped[:, :, :rot_half]
    upper_half = shaped[:, :, rot_half:ROT]
    turned = jnp.concatenate(
        [
            lower_half * cosine_tab - upper_half * sine_tab,
            upper_half * cosine_tab + lower_half * sine_tab,
            shaped[:, :, ROT:],
        ],
        axis=2,
    )
    return turned.reshape(tok_rows, local_heads * HD)


def slice_rows(array, row_start, row_count):
    return lax.dynamic_slice_in_dim(array, row_start, row_count, 0)


def back_norm(gradient, gain_vec, normed_rows, inv_rows):
    scaled = gradient * gain_vec
    centered = scaled - jnp.mean(scaled, axis=1, keepdims=True)
    return inv_rows * (
        centered - normed_rows * jnp.mean(scaled * normed_rows, axis=1, keepdims=True)
    )


def on_device(
    tokens,
    cotangent,
    seq_ids,
    block_slot,
    masters,
    left_stats,
    right_stats,
    left_roots,
    right_roots,
    vectors,
    vector_momentum,
):
    tensor_ways = lax.axis_size("tensor")
    tensor_index = lax.axis_index("tensor")
    data_ways = lax.axis_size("dp")
    data_index = lax.axis_index("dp")
    tok_rows, model_width = tokens.shape
    blk_size = masters.shape[-1]
    slot_count = masters.shape[1]
    local_heads = H // tensor_ways
    width_qkv = 3 * model_width // tensor_ways
    width_heads = model_width // tensor_ways
    width_hidden = FF // tensor_ways
    blocks_qkv = model_width // blk_size * (width_qkv // blk_size)
    blocks_attn = width_heads // blk_size * (model_width // blk_size)
    blocks_in = model_width // blk_size * (width_hidden // blk_size)
    mark_two = blocks_qkv + blocks_attn
    mark_three = mark_two + blocks_in
    copies = masters[0].astype(jnp.bfloat16)
    gathered = lax.all_gather(copies, "dp", axis=0, tiled=True)
    picked = jnp.take(gathered, block_slot, axis=0)
    w_qkv = unblock(picked[:blocks_qkv], model_width, width_qkv)
    w_attn = unblock(picked[blocks_qkv:mark_two], width_heads, model_width)
    w_in = unblock(picked[mark_two:mark_three], model_width, width_hidden)
    w_out = unblock(picked[mark_three:], width_hidden, model_width)
    gain_one = vectors[0:model_width]
    bias_one = vectors[model_width : 2 * model_width]
    gain_two = vectors[2 * model_width : 3 * model_width]
    bias_two = vectors[3 * model_width : 4 * model_width]
    bias_qkv = lax.dynamic_slice_in_dim(
        vectors, 4 * model_width + tensor_index * width_qkv, width_qkv
    )
    bias_attn = vectors[7 * model_width : 8 * model_width]
    bias_in = lax.dynamic_slice_in_dim(
        vectors, 8 * model_width + tensor_index * width_hidden, width_hidden
    )
    bias_out = vectors[8 * model_width + FF : 9 * model_width + FF]
    places = jnp.arange(tok_rows, dtype=jnp.int32)
    seq_first = jnp.concatenate([places[:1] == 0, seq_ids[1:] != seq_ids[:-1]])
    seq_start = lax.cummax(jnp.where(seq_first, places, 0), axis=0)
    position = (places - seq_start).astype(jnp.float32)
    rot_half = ROT // 2
    inverse = 10000.0 ** (-(2.0 * jnp.arange(rot_half, dtype=jnp.float32)) / ROT)
    angles = position[:, None] * inverse[None, :]
    cosine_tab = jnp.cos(angles)[:, None, :]
    sine_tab = jnp.sin(angles)[:, None, :]
    tokens_f = tokens.astype(jnp.float32)
    row_mean = jnp.mean(tokens_f, axis=1, keepdims=True)
    centered = tokens_f - row_mean
    inv_std = lax.rsqrt(jnp.mean(centered * centered, axis=1, keepdims=True) + norm_eps)
    normed = centered * inv_std
    norm_one = (normed * gain_one + bias_one).astype(jnp.bfloat16)
    norm_two = (normed * gain_two + bias_two).astype(jnp.bfloat16)
    mixed_qkv = jnp.dot(norm_one, w_qkv, preferred_element_type=jnp.float32) + bias_qkv
    queries = (
        rotate(mixed_qkv[:, :width_heads], cosine_tab, sine_tab, local_heads)
        .astype(jnp.bfloat16)
        .reshape(tok_rows, local_heads, HD)
    )
    keys_rot = (
        rotate(mixed_qkv[:, width_heads : 2 * width_heads], cosine_tab, sine_tab, local_heads)
        .astype(jnp.bfloat16)
        .reshape(tok_rows, local_heads, HD)
    )
    values_all = (
        mixed_qkv[:, 2 * width_heads :].astype(jnp.bfloat16).reshape(tok_rows, local_heads, HD)
    )
    blk_rows = min(512, tok_rows)
    block_total = tok_rows // blk_rows
    score_scale = HD ** (-0.5)

    def block_scores(block_index):
        row_low = block_index * blk_rows
        row_high = row_low + blk_rows
        scores = (
            jnp.einsum(
                "qhe,khe->hqk",
                queries[row_low:row_high],
                keys_rot[:row_high],
                preferred_element_type=jnp.float32,
            )
            * score_scale
        )
        allowed = (seq_ids[row_low:row_high, None] == seq_ids[None, :row_high]) & (
            places[row_low:row_high, None] >= places[None, :row_high]
        )
        return jnp.where(allowed[None], scores, floor_score)

    outputs = []
    log_sums = []
    for block_index in range(block_total):
        key_span = (block_index + 1) * blk_rows
        scores = block_scores(block_index)
        row_max = jnp.max(scores, axis=2, keepdims=True)
        exp_scores = jnp.exp(scores - row_max)
        row_total = jnp.sum(exp_scores, axis=2, keepdims=True)
        weights_low = (exp_scores / row_total).astype(jnp.bfloat16)
        outputs.append(
            jnp.einsum(
                "hqk,khe->qhe",
                weights_low,
                values_all[:key_span],
                preferred_element_type=jnp.float32,
            )
        )
        log_sums.append(row_max + jnp.log(row_total))
    attended = jnp.concatenate(outputs, axis=0).reshape(tok_rows, width_heads).astype(jnp.bfloat16)
    pre_hidden = jnp.dot(norm_two, w_in, preferred_element_type=jnp.float32) + bias_in
    hidden = jax.nn.gelu(pre_hidden, approximate=False).astype(jnp.bfloat16)
    own_rows = tok_rows // tensor_ways
    row_base = tensor_index * own_rows
    row_start = jnp.int32(0)
    attn_part = slice_rows(attended, row_start, lax.axis_size("tensor") * own_rows)
    hidden_part = slice_rows(hidden, row_start, lax.axis_size("tensor") * own_rows)
    branch_total = lax.psum_scatter(
        (
            jnp.dot(attn_part, w_attn, preferred_element_type=jnp.float32)
            + jnp.dot(hidden_part, w_out, preferred_element_type=jnp.float32)
        ).astype(jnp.bfloat16),
        "tensor",
        scatter_dimension=0,
        tiled=True,
    ).astype(jnp.float32)
    tokens_own = slice_rows(tokens_f, row_base, own_rows)
    mixed = (tokens_own + branch_total + bias_attn + bias_out).astype(jnp.bfloat16)
    grad_out_w = contract(hidden, cotangent, 0, 0)
    grad_hidden = contract(cotangent, w_out, 1, 1)
    density = jnp.exp(-0.5 * pre_hidden * pre_hidden) * 0.3989422804014327
    slope = 0.5 * (1.0 + lax.erf(pre_hidden * 0.7071067811865476)) + pre_hidden * density
    grad_pre = (grad_hidden * slope).astype(jnp.bfloat16)
    grad_in_w = contract(norm_two, grad_pre, 0, 0)
    grad_norm_two = contract(grad_pre, w_in, 1, 1)
    grad_bias_in = jnp.sum(grad_pre.astype(jnp.float32), axis=0)
    grad_attn_w = contract(attended, cotangent, 0, 0)
    grad_attended = (
        contract(cotangent, w_attn, 1, 1).astype(jnp.bfloat16).reshape(tok_rows, local_heads, HD)
    )
    grad_queries = []
    grad_keys = jnp.zeros((tok_rows, local_heads, HD), jnp.float32)
    grad_values = jnp.zeros((tok_rows, local_heads, HD), jnp.float32)
    for block_index in range(block_total):
        row_low = block_index * blk_rows
        row_high = row_low + blk_rows
        scores = block_scores(block_index)
        prob_full = jnp.exp(scores - log_sums[block_index])
        prob_low = prob_full.astype(jnp.bfloat16)
        grad_probs = jnp.einsum(
            "qhe,khe->hqk",
            grad_attended[row_low:row_high],
            values_all[:row_high],
            preferred_element_type=jnp.float32,
        )
        row_delta = jnp.sum(prob_full * grad_probs, axis=2, keepdims=True)
        grad_scores = (prob_full * (grad_probs - row_delta)).astype(jnp.bfloat16)
        grad_queries.append(
            jnp.einsum(
                "hqk,khe->qhe", grad_scores, keys_rot[:row_high], preferred_element_type=jnp.float32
            )
            * score_scale
        )
        grad_keys = grad_keys.at[:row_high].add(
            jnp.einsum(
                "hqk,qhe->khe",
                grad_scores,
                queries[row_low:row_high],
                preferred_element_type=jnp.float32,
            )
            * score_scale
        )
        grad_values = grad_values.at[:row_high].add(
            jnp.einsum(
                "hqk,qhe->khe",
                prob_low,
                grad_attended[row_low:row_high],
                preferred_element_type=jnp.float32,
            )
        )
    grad_query_all = jnp.concatenate(grad_queries, axis=0).reshape(tok_rows, width_heads)
    grad_mixed = jnp.concatenate(
        [
            rotate(grad_query_all, cosine_tab, -sine_tab, local_heads),
            rotate(grad_keys.reshape(tok_rows, width_heads), cosine_tab, -sine_tab, local_heads),
            grad_values.reshape(tok_rows, width_heads),
        ],
        axis=1,
    ).astype(jnp.bfloat16)
    grad_qkv_w = contract(norm_one, grad_mixed, 0, 0)
    grad_norm_one = contract(grad_mixed, w_qkv, 1, 1)
    grad_bias_qkv = jnp.sum(grad_mixed.astype(jnp.float32), axis=0)
    row_start = jnp.int32(0)
    row_count = lax.axis_size("tensor") * own_rows
    normed_rows = slice_rows(normed, row_start, row_count)
    inv_rows = slice_rows(inv_std, row_start, row_count)
    input_part = lax.psum_scatter(
        (
            back_norm(
                slice_rows(grad_norm_one, row_start, row_count), gain_one, normed_rows, inv_rows
            )
            + back_norm(
                slice_rows(grad_norm_two, row_start, row_count), gain_two, normed_rows, inv_rows
            )
        ).astype(jnp.bfloat16),
        "tensor",
        scatter_dimension=0,
        tiled=True,
    ).astype(jnp.float32)
    cot_own = slice_rows(cotangent, row_base, own_rows).astype(jnp.float32)
    input_grad = cot_own + input_part
    bias_grad_out = jnp.sum(cot_own, axis=0)
    pieces = [
        jnp.sum(grad_norm_one * normed, axis=0),
        jnp.sum(grad_norm_one, axis=0),
        jnp.sum(grad_norm_two * normed, axis=0),
        jnp.sum(grad_norm_two, axis=0),
        lax.dynamic_update_slice_in_dim(
            jnp.zeros((3 * model_width,), jnp.float32), grad_bias_qkv, tensor_index * width_qkv, 0
        ),
        bias_grad_out,
        lax.dynamic_update_slice_in_dim(
            jnp.zeros((FF,), jnp.float32), grad_bias_in, tensor_index * width_hidden, 0
        ),
        bias_grad_out,
    ]
    vector_sum = lax.psum(jnp.concatenate(pieces), ("dp", "tensor"))
    grad_scale = 1.0 / jnp.sqrt(jnp.float32(data_ways * tok_rows))
    vector_grad = vector_sum * grad_scale
    new_momentum = decay_vector * vector_momentum + (1.0 - decay_vector) * vector_grad
    new_vectors = vectors - rate_vector * new_momentum
    local_blocks = jnp.concatenate(
        [
            to_blocks(grad_qkv_w, blk_size),
            to_blocks(grad_attn_w, blk_size),
            to_blocks(grad_in_w, blk_size),
            to_blocks(grad_out_w, blk_size),
        ],
        axis=0,
    )
    slot_total = data_ways * slot_count
    summed = lax.psum(local_blocks, "dp")
    owner_of = (
        jnp.full((slot_total,), -1, jnp.int32)
        .at[block_slot]
        .set(jnp.arange(block_slot.shape[0], dtype=jnp.int32))
    )
    mine_blocks = lax.dynamic_slice_in_dim(owner_of, data_index * slot_count, slot_count, 0)
    owned = jnp.where(
        (mine_blocks >= 0)[:, None, None],
        jnp.take(summed, jnp.maximum(mine_blocks, 0), axis=0),
        0.0,
    )
    grad_blocks = owned * grad_scale
    highest = lax.Precision.HIGHEST
    new_left = (
        0.5 * left_stats[0]
        + 0.5 * jnp.einsum("sij,skj->sik", grad_blocks, grad_blocks, precision=highest) / blk_size
    )
    new_right = (
        0.5 * right_stats[0]
        + 0.5 * jnp.einsum("sji,sjk->sik", grad_blocks, grad_blocks, precision=highest) / blk_size
    )
    update_step = jnp.einsum("sij,sjk->sik", left_roots[0], grad_blocks, precision=highest)
    update_step = jnp.einsum("sij,sjk->sik", update_step, right_roots[0], precision=highest)
    new_masters = masters[0] - rate_matrix * update_step
    return (
        mixed,
        input_grad,
        grad_blocks[None],
        new_masters[None],
        new_left[None],
        new_right[None],
        new_vectors,
        new_momentum,
    )


def solution(mesh):
    return jax.shard_map(
        on_device,
        mesh=mesh,
        in_specs=(
            P("dp", None),
            P("dp", None),
            P("dp"),
            P(),
            P("tensor", "dp", None, None),
            P("tensor", "dp", None, None),
            P("tensor", "dp", None, None),
            P("tensor", "dp", None, None),
            P("tensor", "dp", None, None),
            P(),
            P(),
        ),
        out_specs=(
            P(("dp", "tensor"), None),
            P(("dp", "tensor"), None),
            P("tensor", "dp", None, None),
            P("tensor", "dp", None, None),
            P("tensor", "dp", None, None),
            P("tensor", "dp", None, None),
            P(),
            P(),
        ),
        check_vma=False,
    )
```

profile of v0, /device:TPU:0, one launch (start us, length us, event | category | flops | bytes accessed | tf_op | source)
XLA Modules:
  0.0 953.4 jit_solution(12270465933401899179)
XLA Ops:
  28.0 88.9 %all-gather.2.cloned.1.call-done = bf16[224,128,128]{2,1,0:T(8,128)(2,1)} async-done(((bf16[14,128,128]{2,1,0:T(8,128)(2,1)}), bf16[224,128,128]{2,1,0:T(8,128)(2,1)}) %all-gather.2.cloned.1.call-update) | async-done | bytes 7340048 | tf_op jit(solution)/shard_map/all_gather | solution.py:103
  116.9 11.4 %gather_fusion = bf16[216,128,128]{2,1,0:T(8,128)(2,1)} fusion(bf16[224,128,128]{2,1,0:T(8,128)(2,1)} %all-gather.2.cloned.1.call-done, s32[1024]{0:T(1024)S(1)} %pad_clamp_fusion.1), kind=kCustom, calls=%fused_computation | custom fusion | bytes 14156640 | tf_op jit(solution)/shard_map/jit(_take)/gather | solution.py:104
  139.3 6.8 fusion.159
  185.5 6.2 multiply_reduce_fusion.2
  194.5 7.3 multiply_convert_fusion.2
  206.2 8.4 fusion.161
  214.7 9.0 fusion.2
  223.7 10.5 %fusion.53 = f32[2048,6,64]{0,2,1:T(8,128)} fusion(f32[2048,6,64]{0,2,1:T(8,128)} %copy-done.8, bf16[512,6,64]{0,2,1:T(8,128)(2,1)S(1)} %bitcast.244, f32[6,512,1536]{2,1,0:T(8,128)} %get-tuple-element.177, f32[6,512]{1,0:T(8,128)S(1)} %log_add_fusion.1), kind=kOutput, calls=%fused_computation.109 | convolution fusion | flops 614006784 | bytes 23998464 | tf_op jit(solution)/shard_map/hqk,qhe->khe/dot_general | solution.py:254
  234.2 12.1 %multiply_reduce_fusion.1 = (f32[6,512]{1,0:T(8,128)S(1)}, f32[6,512,1536]{2,1,0:T(8,128)}) fusion(f32[6,512,1536]{2,1,0:T(8,128)} %get-tuple-element.177, f32[6,512]{1,0:T(8,128)S(1)} %log_add_fusion.1, bf16[512,6,64]{0,2,1:T(8,128)(2,1)S(1)} %bitcast.245, bf16[1536,6,64]{0,2,1:T(8,128)(2,1)S(1)} %bitcast.241), kind=kOutput, calls=%fused_computation.14 | convolution fusion | flops 618132480 | bytes 39346176 | tf_op jit(solution)/shard_map/qhe,khe->hqk/dot_general | solution.py:230
  246.3 12.9 %multiply_convert_fusion.1 = bf16[6,512,1536]{2,1,0:T(8,128)(2,1)S(1)} fusion(f32[6,512,1536]{2,1,0:T(8,128)} %get-tuple-element.187, f32[6,512,1536]{2,1,0:T(8,128)} %get-tuple-element.177, f32[6,512]{1,0:T(8,128)S(1)} %get-tuple-element.186, f32[6,512]{1,0:T(8,128)S(1)} %log_add_fusion.1), kind=kLoop, calls=%fused_computation.13 | loop fusion | flops 18874368 | bytes 47210496 | tf_op jit(solution)/shard_map/convert_element_type | solution.py:237
  265.9 34.4 %fusion.6 = (bf16[2048,1536]{1,0:T(8,128)(2,1)S(1)}, f32[2048,1536]{1,0:T(8,128)}) fusion(f32[1536]{0:T(1024)S(1)} %copy-done.66, bf16[96,8,12,128]{3,2,1,0:T(8,128)(2,1)S(1)} %bitcast.253, bf16[2048,768]{1,0:T(8,128)(2,1)S(1)} %copy-done.2, f32[768]{0:T(1024)S(1)} %copy-done.70, f32[768]{0:T(1024)S(1)} %copy-done.65, f32[2048]{0:T(1024)S(1)} %add_rsqrt_fusion, ...), kind=kOutput, calls=%fused_computation.24 | convolution fusion | flops 5048893440 | bytes 24408064 | tf_op jit(solution)/shard_map/dot_general | solution.py:191
  300.4 13.2 %convert_reduce_fusion = (f32[1536]{0:T(1024)}, bf16[2048,1536]{1,0:T(8,128)(2,1)S(1)}) fusion(f32[2048,1536]{1,0:T(8,128)} %get-tuple-element.171, f32[1536]{0:T(1024)S(1)} %copy-done.66, bf16[2048,768]{1,0:T(8,128)(2,1)S(1)} %copy-done.19, bf16[192,8,6,128]{3,2,1,0:T(8,128)(2,1)S(1)} %bitcast.255), kind=kOutput, calls=%fused_computation.32 | convolution fusion | flops 4872731136 | bytes 24391680 | tf_op jit(solution)/shard_map/dot_general | solution.py:18
  313.6 7.0 fusion.60
  320.6 6.9 fusion.58
  327.5 10.7 %fusion.160 = (f32[6,512]{1,0:T(8,128)S(1)}, f32[6,512,2048]{2,1,0:T(8,128)}) fusion(bf16[2048,6,64]{0,2,1:T(8,128)(2,1)S(1)} %get-tuple-element.194, bf16[2048,6,64]{0,2,1:T(8,128)(2,1)S(1)} %copy-done.13, pred[512,2048]{1,0:T(8,128)(4,1)S(1)} %copy-done.17), kind=kOutput, calls=%fused_computation.283 | convolution fusion | flops 824177664 | bytes 28192768 | tf_op jit(solution)/shard_map/qhe,khe->hqk/dot_general | solution.py:159
  338.3 10.9 %fusion = f32[6,512]{1,0:T(8,128)S(1)} fusion(f32[6,512,2048]{2,1,0:T(8,128)} %get-tuple-element.175, f32[6,512]{1,0:T(8,128)S(1)} %get-tuple-element.174), kind=kLoop, calls=%fused_computation.9 | loop fusion | flops 12579840 | bytes 25190400 | tf_op jit(solution)/shard_map/reduce_sum | solution.py:179
  349.2 11.9 %fusion.39 = bf16[2048,6,64]{0,2,1:T(8,128)(2,1)} fusion(f32[2048,6,64]{0,2,1:T(8,128)S(1)} %copy-done.9, bf16[512,6,64]{0,2,1:T(8,128)(2,1)S(1)} %bitcast.242, f32[6,512,2048]{2,1,0:T(8,128)} %get-tuple-element.175, f32[6,512]{1,0:T(8,128)S(1)} %log_add_fusion), kind=kOutput, calls=%fused_computation.97 | convolution fusion | flops 819462144 | bytes 30289920 | tf_op jit(solution)/shard_map/hqk,qhe->khe/dot_general | solution.py:254
  361.1 19.5 %multiply_reduce_fusion = (f32[6,512]{1,0:T(8,128)S(1)}, f32[6,512,2048]{2,1,0:T(8,128)}) fusion(f32[6,512,2048]{2,1,0:T(8,128)} %get-tuple-element.175, f32[6,512]{1,0:T(8,128)S(1)} %log_add_fusion, bf16[512,6,64]{0,2,1:T(8,128)(2,1)S(1)} %bitcast.243, bf16[2048,6,64]{0,2,1:T(8,128)(2,1)S(1)} %bitcast.227), kind=kOutput, calls=%fused_computation.4 | convolution fusion | flops 824177664 | bytes 52322304 | tf_op jit(solution)/shard_map/qhe,khe->hqk/dot_general | solution.py:230
  380.6 16.9 %multiply_convert_fusion = bf16[6,512,2048]{2,1,0:T(8,128)(2,1)S(1)} fusion(f32[6,512,2048]{2,1,0:T(8,128)} %get-tuple-element.189, f32[6,512,2048]{2,1,0:T(8,128)} %get-tuple-element.175, f32[6,512]{1,0:T(8,128)S(1)} %get-tuple-element.188, f32[6,512]{1,0:T(8,128)S(1)} %log_add_fusion), kind=kLoop, calls=%fused_computation.3 | loop fusion | flops 25165824 | bytes 62939136 | tf_op jit(solution)/shard_map/convert_element_type | solution.py:237
  412.1 11.4 %multiply_reduce_fusion.4 = (f32[768]{0:T(1024)S(1)}, f32[2048]{0:T(1024)S(1)}, f32[2048]{0:T(1024)S(1)}, f32[768]{0:T(1024)S(1)}, f32[768]{0:T(1024)S(1)}, /*in...) fusion(bf16[2048,768]{1,0:T(8,128)(2,1)S(1)} %copy-done.3, ...), kind=kOutput, calls=%fused_computation.67 | convolution fusion | flops 3664761856 | bytes 22284288 | tf_op jit(solution)/shard_map/dot_general | solution.py:18
  423.6 6.5 multiply_convert_fusion.3
  430.3 9.9 %fusion.100 = bf16[6,64,512]{2,1,0:T(8,128)(2,1)S(1)} fusion(bf16[1536,6,64]{0,2,1:T(8,128)(2,1)} %bitcast.240, f32[6,512,1536]{2,1,0:T(8,128)} %get-tuple-element.177, f32[6,512]{1,0:T(8,128)S(1)} %copy-done.59, f32[6,512]{1,0:T(8,128)S(1)} %copy-done.57), kind=kOutput, calls=%fused_computation.169 | convolution fusion | flops 618332160 | bytes 20471808 | tf_op jit(solution)/shard_map/hqk,khe->qhe/dot_general | solution.py:182
  440.2 10.7 %fusion.101 = bf16[6,64,512]{2,1,0:T(8,128)(2,1)S(1)} fusion(bf16[2048,6,64]{0,2,1:T(8,128)(2,1)S(1)} %bitcast.228, f32[6,512,2048]{2,1,0:T(8,128)} %get-tuple-element.175, f32[6,512]{1,0:T(8,128)S(1)} %fusion, f32[6,512]{1,0:T(8,128)S(1)} %get-tuple-element.174), kind=kOutput, calls=%fused_computation.170 | convolution fusion | flops 824377344 | bytes 27156480 | tf_op jit(solution)/shard_map/hqk,khe->qhe/dot_general | solution.py:182
  460.3 11.8 %fusion.153 = f32[768,1536]{1,0:T(8,128)} fusion(bf16[2048,1536]{1,0:T(8,128)(2,1)} %copy-done.74, bf16[2048,768]{1,0:T(8,128)(2,1)} %param.31, f32[768]{0:T(1024)S(1)} %copy-done.71, f32[768]{0:T(1024)S(1)} %copy-done.65, f32[2048]{0:T(1024)S(1)} %add_rsqrt_fusion, f32[2048]{0:T(1024)S(1)} %broadcast_multiply_fusion.4), kind=kOutput, calls=%fused_computation.276 | convolution fusion | flops 4841275392 | bytes 14178304 | tf_op jit(solution)/shard_map/dot_general | solution.py:18
  472.1 6.7 reshape.811
  478.8 6.7 copy.53
  485.4 8.7 fusion.165
  494.1 6.8 reshape.813
  506.9 6.1 fusion.152
  528.8 7.8 pad_maximum_fusion
  551.0 42.9 %psum.15 = f32[9984]{0:T(1024)S(1)} all-reduce(f32[9984]{0:T(1024)S(1)} %constant_dynamic-update-slice_fusion), channel_id=1, replica_groups=mesh['dp'=16,'tensor'=2] {'dp','tensor'}, use_global_device_ids=true, to_apply=%region_31.32 | all-reduce | flops 9984 | bytes 79872 | tf_op jit(solution)/shard_map/psum | solution.py:307
  598.7 329.6 %all-reduce.4.cloned.1.call-done = f32[216,128,128]{2,1,0:T(8,128)} async-done(((f32[216,128,128]{2,1,0:T(8,128)}), f32[216,128,128]{2,1,0:T(8,128)}) %all-reduce.4.cloned.1.call-update) | async-done | bytes 14155792 | tf_op jit(solution)/shard_map/psum | solution.py:322
  (299 shorter events, 167.2 us)
Async XLA Ops:
  7.2 936.1 %copy-start = (f32[1,14,128,128]{3,2,1,0:T(8,128)S(1)}, f32[1,14,128,128]{3,2,1,0:T(8,128)}, u32[]{:S(2)}) copy-start(f32[1,14,128,128]{3,2,1,0:T(8,128)} %param.38) | copy-start | bytes 2752516
  7.2 14.8 %slice-start.5 = ((s32[2048]{0:T(1024)}), s32[1024]{0:T(1024)S(1)}, s32[]{:S(2)}) async-start(s32[2048]{0:T(1024)} %param.33), calls=%async_computation.11 | async-start | bytes 8192 | tf_op jit(solution)/shard_map/slice | solution.py:167
  7.2 17.1 %copy-start.53 = (s32[2048]{0:T(1024)S(1)}, s32[2048]{0:T(1024)}, u32[]{:S(2)}) copy-start(s32[2048]{0:T(1024)} %param.33) | copy-start | bytes 24580
  7.2 13.9 %copy-start.54 = (f32[9984]{0:T(1024)S(1)}, f32[9984]{0:T(1024)}, u32[]{:S(2)}) copy-start(f32[9984]{0:T(1024)} %param.40) | copy-start | bytes 119812
  7.2 109.7 %all-gather.2.cloned.1.call-start = ((), (), s32[]{:S(2)}) async-start(), calls=%async_computation.2 | async-start | bytes 7798784 | tf_op jit(solution)/shard_map/all_gather | solution.py:103
  9.4 537.5 %reduce-scatter.5.cloned.1.call-start = ((), (), s32[]{:S(2)}) async-start(), calls=%async_computation.4 | async-start | bytes 4718592 | tf_op jit(solution)/shard_map/reduce_scatter | solution.py:277
  21.7 117.6 %copy-start.63 = (f32[768]{0:T(1024)}, f32[768]{0:T(1024)S(1)}, u32[]{:S(2)}) copy-start(f32[768]{0:T(1024)S(1)} %get-tuple-element.160) | copy-start | bytes 9220
  21.7 117.6 %copy-start.68 = (f32[768]{0:T(1024)}, f32[768]{0:T(1024)S(1)}, u32[]{:S(2)}) copy-start(f32[768]{0:T(1024)S(1)} %get-tuple-element.159) | copy-start | bytes 9220
  24.2 123.0 %copy-start.43 = (f32[2048,8]{0,1:T(8,128)}, f32[2048,8]{0,1:T(8,128)S(1)}, u32[]{:S(2)}) copy-start(f32[2048,8]{0,1:T(8,128)S(1)} %get-tuple-element.164) | copy-start | bytes 196612
  154.1 173.4 %copy-start.1 = (bf16[2048,6,64]{0,2,1:T(8,128)(2,1)}, bf16[2048,6,64]{0,2,1:T(8,128)(2,1)S(1)}, u32[]{:S(2)}) copy-start(bf16[2048,6,64]{0,2,1:T(8,128)(2,1)S(1)} %get-tuple-element.194) | copy-start | bytes 4718596
  264.9 35.5 %copy-start.7 = (f32[2048,6,64]{0,2,1:T(8,128)}, f32[2048,6,64]{0,2,1:T(8,128)S(1)}, u32[]{:S(2)}) copy-start(f32[2048,6,64]{0,2,1:T(8,128)S(1)} %fusion.46) | copy-start | bytes 9437188
  265.9 34.5 %copy-start.19 = (bf16[2048,768]{1,0:T(8,128)(2,1)S(1)}, bf16[2048,768]{1,0:T(8,128)(2,1)}, u32[]{:S(2)}) copy-start(bf16[2048,768]{1,0:T(8,128)(2,1)} %param.32) | copy-start | bytes 9437188
  265.9 34.5 %copy-start.38 = (bf16[12,6,128,128]{3,1,2,0:T(8,128)(2,1)S(1)}, bf16[12,6,128,128]{3,1,2,0:T(8,128)(2,1)}, u32[]{:S(2)}) copy-start(bf16[12,6,128,128]{3,1,2,0:T(8,128)(2,1)} %copy.45) | copy-start | bytes 7077892
  300.4 20.2 %copy-start.73 = (bf16[2048,1536]{1,0:T(8,128)(2,1)}, bf16[2048,1536]{1,0:T(8,128)(2,1)S(1)}, u32[]{:S(2)}) copy-start(bf16[2048,1536]{1,0:T(8,128)(2,1)S(1)} %get-tuple-element.170) | copy-start | bytes 18874372
  338.3 10.9 %copy-start.31 = (bf16[512,384]{0,1:T(8,128)(2,1)S(1)}, bf16[512,384]{0,1:T(8,128)(2,1)}, u32[]{:S(2)}) copy-start(bf16[512,384]{0,1:T(8,128)(2,1)} %get-tuple-element.150) | copy-start | bytes 1179652
  349.2 12.0 %copy-start.21 = (bf16[2048,384]{0,1:T(8,128)(2,1)S(1)}, bf16[2048,384]{0,1:T(8,128)(2,1)}, u32[]{:S(2)}) copy-start(bf16[2048,384]{0,1:T(8,128)(2,1)} %slice.514) | copy-start | bytes 4718596
  408.5 15.1 %slice-start.3 = ((s8[6291456]{0:T(1024)(128)(4,1)}), s8[4194304]{0:T(1024)(128)(4,1)S(1)}, s32[]{:S(2)}) async-start(s8[6291456]{0:T(1024)(128)(4,1)} %bitcast.232), calls=%async_computation.9 | async-start | bytes 8388608
  408.6 14.9 %copy-start.25 = (bf16[2048,6,64]{0,2,1:T(8,128)(2,1)}, bf16[2048,6,64]{0,2,1:T(8,128)(2,1)S(1)}, u32[]{:S(2)}) copy-start(bf16[2048,6,64]{0,2,1:T(8,128)(2,1)S(1)} %pad_maximum_fusion.4) | copy-start | bytes 4718596
  408.8 14.7 %copy-start.27 = (bf16[2048,6,64]{0,2,1:T(8,128)(2,1)}, bf16[2048,6,64]{0,2,1:T(8,128)(2,1)S(1)}, u32[]{:S(2)}) copy-start(bf16[2048,6,64]{0,2,1:T(8,128)(2,1)S(1)} %pad_maximum_fusion.5) | copy-start | bytes 4718596
  412.1 11.4 %slice-start.4 = ((s8[6291456]{0:T(1024)(128)(4,1)}), s8[2097152]{0:T(1024)(128)(4,1)S(1)}, s32[]{:S(2)}) async-start(s8[6291456]{0:T(1024)(128)(4,1)} %bitcast.232), calls=%async_computation.10 | async-start | bytes 4194304
  430.2 163.7 %reduce-scatter.3.cloned.1.call-start = ((), (), s32[]{:S(2)}) async-start(), calls=%async_computation.3 | async-start | bytes 4718592 | tf_op jit(solution)/shard_map/reduce_scatter | solution.py:198
  430.2 21.4 %slice-start.6 = ((s8[6291456]{0:T(1024)(128)(4,1)}), s8[4194304]{0:T(1024)(128)(4,1)S(1)}, s32[]{:S(2)}) async-start(s8[6291456]{0:T(1024)(128)(4,1)} %bitcast.274), calls=%async_computation.12 | async-start | bytes 8388608
  440.2 11.5 %copy-start.47 = (bf16[3,6,128,128]{3,1,2,0:T(8,128)(2,1)S(1)}, bf16[3,6,128,128]{3,1,2,0:T(8,128)(2,1)}, u32[]{:S(2)}) copy-start(bf16[3,6,128,128]{3,1,2,0:T(8,128)(2,1)} %copy-done.46) | copy-start | bytes 1769476
  440.2 11.5 %copy-start.48 = (bf16[6,64,512]{2,1,0:T(8,128)(2,1)S(1)}, bf16[6,64,512]{2,1,0:T(8,128)(2,1)}, u32[]{:S(2)}) copy-start(bf16[6,64,512]{2,1,0:T(8,128)(2,1)} %fusion.98) | copy-start | bytes 1179652
  440.2 11.5 %copy-start.49 = (bf16[6,64,512]{2,1,0:T(8,128)(2,1)S(1)}, bf16[6,64,512]{2,1,0:T(8,128)(2,1)}, u32[]{:S(2)}) copy-start(bf16[6,64,512]{2,1,0:T(8,128)(2,1)} %fusion.99) | copy-start | bytes 1179652
  440.2 11.5 %slice-start.7 = ((s8[6291456]{0:T(1024)(128)(4,1)}), s8[2097152]{0:T(1024)(128)(4,1)S(1)}, s32[]{:S(2)}) async-start(s8[6291456]{0:T(1024)(128)(4,1)} %bitcast.274), calls=%async_computation.13 | async-start | bytes 4194304
  455.3 472.9 %all-reduce.4.cloned.1.call-start = ((), (), s32[]{:S(2)}) async-start(), calls=%async_computation.5 | async-start | bytes 28311552 | tf_op jit(solution)/shard_map/psum | solution.py:322
  542.3 51.6 %copy-start.61 = (f32[768]{0:T(1024)S(1)}, f32[768]{0:T(1024)}, u32[]{:S(2)}) copy-start(f32[768]{0:T(1024)} %get-tuple-element.156) | copy-start | bytes 9220
  542.3 51.7 %copy-start.62 = (f32[768]{0:T(1024)S(1)}, f32[768]{0:T(1024)}, u32[]{:S(2)}) copy-start(f32[768]{0:T(1024)} %get-tuple-element.161) | copy-start | bytes 9220
  546.9 51.1 %copy-start.55 = (f32[9984]{0:T(1024)S(1)}, f32[9984]{0:T(1024)}, u32[]{:S(2)}) copy-start(f32[9984]{0:T(1024)} %param.40) | copy-start | bytes 119812
  546.9 51.1 %copy-start.60 = (f32[9984]{0:T(1024)S(1)}, f32[9984]{0:T(1024)}, u32[]{:S(2)}) copy-start(f32[9984]{0:T(1024)} %param.41) | copy-start | bytes 119812
  598.0 346.4 %copy-start.30 = (f32[1,14,128,128]{3,2,1,0:T(8,128)S(1)}, f32[1,14,128,128]{3,2,1,0:T(8,128)}, u32[]{:S(2)}) copy-start(f32[1,14,128,128]{3,2,1,0:T(8,128)} %param.35) | copy-start | bytes 2752516
  (55 other events, 281.3 us)
Sparse Core Ops, SparseCore 0:
  11.3 105.5 all-gather.1
  430.3 9.4 reduce-scatter.4
  455.4 9.4 reduce-scatter.2
  536.8 391.3 all-reduce.3
where the time goes:
time: 962 us; the launch traced here: 953 us
  waiting for transfers between devices  419 us (44%)
  matrix products  267 us (28%)
  other arithmetic  119 us (12%)
  local copies, waits for them, and re-layouts  90.4 us (9%)
  blocking collectives  42.9 us (4%)
  between operations  15.6 us (2%)
    psum x1, waiting for transfers between devices, on_device(): summed = lax.psum(local_blocks, 'dp')  330 us
    all_gather x1, waiting for transfers between devices, on_device(): gathered = lax.all_gather(copies, 'dp', axis=0, tiled=True)  88.9 us
    dot_general x8, matrix products, contract(): lax.dot_general(first_op, second_op, (((first_dim,), (second_dim,)), ((),...  63.7 us
    psum x1, blocking collectives, on_device(): vector_sum = lax.psum(jnp.concatenate(pieces), ('dp', 'tensor'))  42.9 us
    convert_element_type x4, other arithmetic, on_device(): grad_scores = (prob_full * (grad_probs - row_delta)).astype(jnp.bfloat16)  39.5 us
    dot_general x4, matrix products, on_device(): jnp.einsum('qhe,khe->hqk', grad_attended[row_low:row_high], values_all[:r...  39.1 us
    dot_general x1, matrix products, on_device(): jnp.dot(norm_two, w_in, preferred_element_type=jnp.float32) + bias_in  34.4 us
    dot_general x4, matrix products, on_device(): jnp.einsum('hqk,qhe->khe', prob_low, grad_attended[row_low:row_high], pre...  27.2 us
  transfers between devices with their start and end apart: 4, of which 2 were waited for; matrix products, arithmetic and copies ran while one was open for 15% of the time, Pallas kernels for 0%

commit v1 on v0

--- a/solution.py
+++ b/solution.py
@@ -319,7 +319,12 @@
         axis=0,
     )
     slot_total = data_ways * slot_count
-    summed = lax.psum(local_blocks, "dp")
+    count_all = jax.lax.axis_size("dp")
+    summed = local_blocks
+    for k in [jj for jj in (1, 2, 4, 8, 16) if jj < count_all]:
+        summed = summed + jax.lax.ppermute(
+            summed, axis_name="dp", perm=[(p, p ^ k) for p in range(count_all)]
+        )
     owner_of = (
         jnp.full((slot_total,), -1, jnp.int32)
         .at[block_slot]

time: 962 us -> 2120 us (2.20)
  blocking collectives: 42.9 us -> 596 us
  waiting for transfers between devices: 419 us -> 968 us
  other arithmetic: 119 us -> 156 us
    ppermute x0 -> x4, waiting for transfers between devices: none -> 881 us  [on_device(): jax.lax.ppermute(summed, axis_name='dp', perm=[(p, p ^ k) for p in range(...]
    psum x1, blocking collectives: 42.9 us -> 596 us  [on_device(): vector_sum = lax.psum(jnp.concatenate(pieces), ('dp', 'tensor'))]
    psum x1 -> x0, waiting for transfers between devices: 330 us -> none  [on_device(): summed = lax.psum(local_blocks, 'dp')]
    add x0 -> x4, other arithmetic: none -> 45.4 us  [on_device(): summed + jax.lax.ppermute(summed, axis_name='dp', perm=[(p, p ^ k) for p...]
  transfers between devices with their start and end apart: 4 -> 7, of which waited for: 2 -> 4; matrix products, arithmetic and copies ran while one was open for 15% -> 4% of each run, Pallas kernels for 0% -> 0%
where the time goes in v1:
time: 2120 us; the launch traced here: 2110 us
  waiting for transfers between devices  968 us (46%)
  blocking collectives  596 us (28%)
  matrix products  268 us (13%)
  other arithmetic  156 us (7%)
  local copies, waits for them, and re-layouts  95.7 us (5%)
    ppermute x4, waiting for transfers between devices, on_device(): jax.lax.ppermute(summed, axis_name='dp', perm=[(p, p ^ k) for p in range(...  881 us
    psum x1, blocking collectives, on_device(): vector_sum = lax.psum(jnp.concatenate(pieces), ('dp', 'tensor'))  596 us
    all_gather x1, waiting for transfers between devices, on_device(): gathered = lax.all_gather(copies, 'dp', axis=0, tiled=True)  86.3 us
    dot_general x8, matrix products, contract(): lax.dot_general(first_op, second_op, (((first_dim,), (second_dim,)), ((),...  61.3 us
    add x4, other arithmetic, on_device(): summed + jax.lax.ppermute(summed, axis_name='dp', perm=[(p, p ^ k) for p...  45.4 us
  transfers between devices with their start and end apart: 7, of which 4 were waited for; matrix products, arithmetic and copies ran while one was open for 4% of the time, Pallas kernels for 0%

profile of v1, /device:TPU:0, one launch (start us, length us, event | category | flops | bytes accessed | tf_op | source)
XLA Modules:
  0.0 2107.5 jit_solution(10009426801010195366)
XLA Ops:
  30.6 86.3 %all-gather.2.cloned.1.call-done = bf16[224,128,128]{2,1,0:T(8,128)(2,1)} async-done(((bf16[14,128,128]{2,1,0:T(8,128)(2,1)}), bf16[224,128,128]{2,1,0:T(8,128)(2,1)}) %all-gather.2.cloned.1.call-update) | async-done | bytes 7340048 | tf_op jit(solution)/shard_map/all_gather | solution.py:103
  116.9 11.4 gather_fusion
  139.3 6.8 fusion.160
  194.4 7.3 multiply_convert_fusion.2
  206.1 8.5 fusion.162
  214.6 9.0 fusion.2
  223.6 9.4 fusion.100
  233.0 12.5 multiply_reduce_fusion.1
  245.5 8.1 fusion.53
  255.2 12.9 multiply_convert_fusion.1
  275.0 34.9 %fusion.6 = (bf16[2048,1536]{1,0:T(8,128)(2,1)}, f32[2048,1536]{1,0:T(8,128)}) fusion(f32[1536]{0:T(1024)S(1)} %copy-done.68, bf16[96,8,12,128]{3,2,1,0:T(8,128)(2,1)S(1)} %bitcast.264, bf16[2048,768]{1,0:T(8,128)(2,1)S(1)} %copy-done.3, f32[768]{0:T(1024)S(1)} %copy-done.71, f32[768]{0:T(1024)S(1)} %copy-done.63, f32[2048]{0:T(1024)S(1)} %copy-done.60, ...), kind=kOutput, calls=%fused_computation.24 | convolution fusion | flops 5048893440 | bytes 24408064 | tf_op jit(solution)/shard_map/dot_general | solution.py:191
  310.0 11.6 convert_reduce_fusion
  324.2 7.3 fusion.153
  331.5 6.7 reshape.811
  344.7 8.7 fusion.166
  365.9 11.7 fusion.161
  377.6 10.5 fusion
  388.2 11.8 fusion.101
  399.9 19.5 multiply_reduce_fusion
  419.4 12.6 fusion.39
  432.1 16.7 multiply_convert_fusion
  490.7 303.0 %collective-permute-done = f32[216,128,128]{2,1,0:T(8,128)} collective-permute-done((f32[216,128,128]{2,1,0:T(8,128)S(1)}, f32[216,128,128]{2,1,0:T(8,128)}, u32[]{:S(2)}, u32[]{:S(2)}) %collective-permute-start) | collective-permute-done | bytes 14155808 | tf_op jit(solution)/shard_map/ppermute | solution.py:325
  793.8 8.5 fusion.154
  808.1 297.9 %collective-permute-done.1 = f32[216,128,128]{2,1,0:T(8,128)} collective-permute-done((f32[216,128,128]{2,1,0:T(8,128)S(1)}, f32[216,128,128]{2,1,0:T(8,128)}, u32[]{:S(2)}, u32[]{:S(2)}) %collective-permute-start.1) | collective-permute-done | bytes 14155808 | tf_op jit(solution)/shard_map/ppermute | solution.py:325
  1106.0 10.3 add.292
  1116.4 9.9 fusion.60
  1126.4 12.3 multiply_reduce_fusion.4
  1138.7 280.4 %collective-permute-done.2 = f32[216,128,128]{2,1,0:T(8,128)} collective-permute-done((f32[216,128,128]{2,1,0:T(8,128)S(1)}, f32[216,128,128]{2,1,0:T(8,128)}, u32[]{:S(2)}, u32[]{:S(2)}) %collective-permute-start.2) | collective-permute-done | bytes 14155808 | tf_op jit(solution)/shard_map/ppermute | solution.py:325
  1419.1 12.1 add.293
  1440.4 8.5 fusion.58
  1466.7 596.3 %psum.7 = f32[9984]{0:T(1024)S(1)} all-reduce(f32[9984]{0:T(1024)S(1)} %constant_dynamic-update-slice_fusion), channel_id=1, replica_groups=mesh['dp'=16,'tensor'=2] {'dp','tensor'}, use_global_device_ids=true, to_apply=%region_30.31 | all-reduce | flops 9984 | bytes 79872 | tf_op jit(solution)/shard_map/psum | solution.py:307
  2067.6 14.6 add.294
  (313 shorter events, 213.9 us)
Async XLA Ops:
  7.2 2090.2 %copy-start = (f32[1,14,128,128]{3,2,1,0:T(8,128)S(1)}, f32[1,14,128,128]{3,2,1,0:T(8,128)}, u32[]{:S(2)}) copy-start(f32[1,14,128,128]{3,2,1,0:T(8,128)} %param.38) | copy-start | bytes 2752516
  7.2 109.7 %all-gather.2.cloned.1.call-start = ((), (), s32[]{:S(2)}) async-start(), calls=%async_computation.2 | async-start | bytes 7798784 | tf_op jit(solution)/shard_map/all_gather | solution.py:103
  9.4 1453.0 %reduce-scatter.5.cloned.1.call-start = ((), (), s32[]{:S(2)}) async-start(), calls=%async_computation.4 | async-start | bytes 4718592 | tf_op jit(solution)/shard_map/reduce_scatter | solution.py:277
  12.9 11.6 slice-start.9
  20.4 118.8 %copy-start.56 = (f32[2048]{0:T(1024)}, f32[2048]{0:T(1024)S(1)}, u32[]{:S(2)}) copy-start(f32[2048]{0:T(1024)S(1)} %broadcast_multiply_fusion.4) | copy-start | bytes 24580
  23.5 115.7 %copy-start.59 = (f32[2048]{0:T(1024)}, f32[2048]{0:T(1024)S(1)}, u32[]{:S(2)}) copy-start(f32[2048]{0:T(1024)S(1)} %add_rsqrt_fusion) | copy-start | bytes 24580
  24.2 115.0 %copy-start.65 = (f32[768]{0:T(1024)}, f32[768]{0:T(1024)S(1)}, u32[]{:S(2)}) copy-start(f32[768]{0:T(1024)S(1)} %get-tuple-element.160) | copy-start | bytes 9220
  24.2 115.0 %copy-start.69 = (f32[768]{0:T(1024)}, f32[768]{0:T(1024)S(1)}, u32[]{:S(2)}) copy-start(f32[768]{0:T(1024)S(1)} %get-tuple-element.159) | copy-start | bytes 9220
  26.8 120.4 %copy-start.41 = (f32[2048,8]{0,1:T(8,128)}, f32[2048,8]{0,1:T(8,128)S(1)}, u32[]{:S(2)}) copy-start(f32[2048,8]{0,1:T(8,128)S(1)} %get-tuple-element.164) | copy-start | bytes 196612
  154.1 211.8 %copy-start.1 = (bf16[2048,6,64]{0,2,1:T(8,128)(2,1)}, bf16[2048,6,64]{0,2,1:T(8,128)(2,1)S(1)}, u32[]{:S(2)}) copy-start(bf16[2048,6,64]{0,2,1:T(8,128)(2,1)S(1)} %get-tuple-element.194) | copy-start | bytes 4718596
  233.0 12.5 copy-start.10
  274.9 35.0 %copy-start.8 = (f32[2048,6,64]{0,2,1:T(8,128)}, f32[2048,6,64]{0,2,1:T(8,128)S(1)}, u32[]{:S(2)}) copy-start(f32[2048,6,64]{0,2,1:T(8,128)S(1)} %fusion.46) | copy-start | bytes 9437188
  275.0 35.0 %copy-start.20 = (bf16[2048,768]{1,0:T(8,128)(2,1)S(1)}, bf16[2048,768]{1,0:T(8,128)(2,1)}, u32[]{:S(2)}) copy-start(bf16[2048,768]{1,0:T(8,128)(2,1)} %param.32) | copy-start | bytes 9437188
  275.0 35.0 %copy-start.35 = (bf16[12,6,128,128]{3,1,2,0:T(8,128)(2,1)S(1)}, bf16[12,6,128,128]{3,1,2,0:T(8,128)(2,1)}, u32[]{:S(2)}) copy-start(bf16[12,6,128,128]{3,1,2,0:T(8,128)(2,1)} %copy.45) | copy-start | bytes 7077892
  388.2 11.8 copy-start.29
  480.5 313.3 %slice-start.2 = ((s8[4718592]{0:T(1024)(128)(4,1)}), s8[4194304]{0:T(1024)(128)(4,1)S(1)}, s32[]{:S(2)}) async-start(s8[4718592]{0:T(1024)(128)(4,1)} %bitcast.216), calls=%async_computation.7 | async-start | bytes 8388608
  484.6 309.1 %slice-start.3 = ((s8[4718592]{0:T(1024)(128)(4,1)}), s8[524288]{0:T(1024)(128)(4,1)S(1)}, s32[]{:S(2)}) async-start(s8[4718592]{0:T(1024)(128)(4,1)} %bitcast.216), calls=%async_computation.8 | async-start | bytes 1048576
  489.2 304.5 %collective-permute-start = (f32[216,128,128]{2,1,0:T(8,128)S(1)}, f32[216,128,128]{2,1,0:T(8,128)}, u32[]{:S(2)}, u32[]{:S(2)}) collective-permute-start(f32[216,128,128]{2,1,0:T(8,128)S(1)} %pad_maximum_fusion), channel_id=1, source_target_pairs={{0,2},{2,0},{4,6},{6,4},{8,10},{10,8},{12,14},{14,12},{16,18},{18,... | collective-permute-start | bytes 42467336 | tf_op jit(solution)/shard_map/ppermute | solution.py:325
  802.3 314.1 %copy-start.37 = (bf16[6,12,128,128]{3,1,2,0:T(8,128)(2,1)S(1)}, bf16[6,12,128,128]{3,1,2,0:T(8,128)(2,1)}, u32[]{:S(2)}) copy-start(bf16[6,12,128,128]{3,1,2,0:T(8,128)(2,1)} %copy.44) | copy-start | bytes 7077892
  802.3 303.7 %collective-permute-start.1 = (f32[216,128,128]{2,1,0:T(8,128)S(1)}, f32[216,128,128]{2,1,0:T(8,128)}, u32[]{:S(2)}, u32[]{:S(2)}) collective-permute-start(f32[216,128,128]{2,1,0:T(8,128)S(1)} %fusion.154), channel_id=1, source_target_pairs={{0,4},{2,6},{4,0},{6,2},{8,12},{10,14},{12,8},{14,10},{16,20},{18,... | collective-permute-start | bytes 42467336 | tf_op jit(solution)/shard_map/ppermute | solution.py:325
  1116.3 302.8 %collective-permute-start.2 = (f32[216,128,128]{2,1,0:T(8,128)S(1)}, f32[216,128,128]{2,1,0:T(8,128)}, u32[]{:S(2)}, u32[]{:S(2)}) collective-permute-start(f32[216,128,128]{2,1,0:T(8,128)S(1)} %add.292), channel_id=1, source_target_pairs={{0,8},{2,10},{4,12},{6,14},{8,0},{10,2},{12,4},{14,6},{16,24},{18,... | collective-permute-start | bytes 42467336 | tf_op jit(solution)/shard_map/ppermute | solution.py:325
  1138.7 297.4 %slice-start.5 = ((s8[6291456]{0:T(1024)(128)(4,1)}), s8[4194304]{0:T(1024)(128)(4,1)S(1)}, s32[]{:S(2)}) async-start(s8[6291456]{0:T(1024)(128)(4,1)} %bitcast.237), calls=%async_computation.10 | async-start | bytes 8388608
  1138.7 297.4 %slice-start.7 = ((s8[6291456]{0:T(1024)(128)(4,1)}), s8[4194304]{0:T(1024)(128)(4,1)S(1)}, s32[]{:S(2)}) async-start(s8[6291456]{0:T(1024)(128)(4,1)} %bitcast.239), calls=%async_computation.12 | async-start | bytes 8388608
  1138.7 297.3 %slice-start.6 = ((s8[6291456]{0:T(1024)(128)(4,1)}), s8[2097152]{0:T(1024)(128)(4,1)S(1)}, s32[]{:S(2)}) async-start(s8[6291456]{0:T(1024)(128)(4,1)} %bitcast.237), calls=%async_computation.11 | async-start | bytes 4194304
  1138.7 297.3 %slice-start.8 = ((s8[6291456]{0:T(1024)(128)(4,1)}), s8[2097152]{0:T(1024)(128)(4,1)S(1)}, s32[]{:S(2)}) async-start(s8[6291456]{0:T(1024)(128)(4,1)} %bitcast.239), calls=%async_computation.13 | async-start | bytes 4194304
  1431.2 636.5 %collective-permute-start.3 = (f32[216,128,128]{2,1,0:T(8,128)}, f32[216,128,128]{2,1,0:T(8,128)}, u32[]{:S(2)}, u32[]{:S(2)}) collective-permute-start(f32[216,128,128]{2,1,0:T(8,128)} %add.293), channel_id=1, source_target_pairs={{0,16},{2,18},{4,20},{6,22},{8,24},{10,26},{12,28},{14,30},{16,0},... | collective-permute-start | bytes 42467336 | tf_op jit(solution)/shard_map/ppermute | solution.py:325
  1440.3 622.6 %reduce-scatter.3.cloned.1.call-start = ((), (), s32[]{:S(2)}) async-start(), calls=%async_computation.3 | async-start | bytes 4718592 | tf_op jit(solution)/shard_map/reduce_scatter | solution.py:198
  1457.7 605.3 %copy-start.61 = (f32[768]{0:T(1024)S(1)}, f32[768]{0:T(1024)}, u32[]{:S(2)}) copy-start(f32[768]{0:T(1024)} %get-tuple-element.156) | copy-start | bytes 9220
  1457.7 605.3 %copy-start.62 = (f32[768]{0:T(1024)S(1)}, f32[768]{0:T(1024)}, u32[]{:S(2)}) copy-start(f32[768]{0:T(1024)} %get-tuple-element.161) | copy-start | bytes 9220
  1462.3 604.7 %copy-start.55 = (f32[9984]{0:T(1024)S(1)}, f32[9984]{0:T(1024)}, u32[]{:S(2)}) copy-start(f32[9984]{0:T(1024)} %param.40) | copy-start | bytes 119812
  1462.3 604.7 %copy-start.58 = (f32[9984]{0:T(1024)S(1)}, f32[9984]{0:T(1024)}, u32[]{:S(2)}) copy-start(f32[9984]{0:T(1024)} %param.41) | copy-start | bytes 119812
  2082.2 16.3 copy-start.28
  (60 other events, 326.2 us)
Sparse Core Ops, SparseCore 0:
  11.3 105.5 all-gather.1
  1440.4 9.5 reduce-scatter.4
  1452.8 11.9 reduce-scatter.2
